TPU v7x, 128 devices: a whole 4x4x4 slice. The times are simulated.
128 devices in a mesh: blk: 32 (over x, y, core), mp: 4 (over z).
Axes of the slice: x: 4, y: 4, z: 4, core: 2. Of those that a mesh axis runs over, the one named last changes fastest.
Arguments:
- hidden: bfloat16 [144, 3584], replicated, may hold values from -6 to 6
- medusa_w: bfloat16 [2, 3584, 3584], P(None, 'blk', 'mp'), may hold values from -0.09375 to 0.09375
- embedding: bfloat16 [131072, 3584], P(('blk', 'mp')), may hold values from -0.5 to 0.5
- cand_ids: int32 [2, 144, 10], replicated, may hold values from 0 to 131071
- tree_q: bfloat16 [12, 48, 4096], P(None, None, 'mp'), may hold values from -6 to 6
- tree_key_value: bfloat16 [2, 12, 48, 2048], P(None, None, None, 'mp'), may hold values from -6 to 6
- prompt_key_value: bfloat16 [2, 32, 2048, 2048], P(None, 'blk', None, 'mp'), may hold values from -6 to 6
- block_group: int32 [32], P('blk'), may hold values from 0 to 11, as said below
- block_len: int32 [32], P('blk'), may hold values from 1 to 2048
- block_empty: int32 [32], P('blk'), may hold values 0 or 1
- parents: int32 [12, 48], replicated, may hold values from 0 to 46, as said below
- out_weight: bfloat16 [4096, 3584], P('mp'), may hold values from -0.09375 to 0.09375
- post_gain: float32 [3584], replicated, may hold values from 0.5 to 1.5
- resid: bfloat16 [576, 3584], P('blk'), may hold values from -6 to 6
Outputs:
- draft_logprob: float32 [2, 144, 10], replicated
- layer_out: bfloat16 [576, 3584], P('blk')
Inputs may be any that keep to these rules, and one draw needn't show every extreme that they name: `block_group`: every group number from 0 to min(12, 32) - 1 owns at least one block. `parents`: entry 0 of each row is 0; entry i for i >= 1 is below i; some group's last token has parent 48 - 2.
All inputs are finite; a program needn't handle non-finite values. No bound on the sum of `block_empty` on one device may be relied on, other than what follows from the above.
Results may differ from a plain program's by a relative error of at most 0.005.
Values may be sent and summed in bfloat16 or wider, within the bound.
A program may use at most 128 MiB of HBM per device.

v0:
```python
import jax
import jax.numpy as jnp
from jax import lax
from jax.sharding import PartitionSpec as P

HEAD_SIZE = 256


def capped(values, limit):
    return limit * jnp.tanh(values / limit)


def ancestry(parents):
    count = parents.shape[1]
    column = jnp.arange(count, dtype=jnp.int32)
    linked = (parents[:, :, None] == column[None, None, :]) & (column[None, :, None] > 0)
    reach = jnp.eye(count, dtype=jnp.float32)[None] + linked.astype(jnp.float32)
    for sweep in range(count.bit_length()):
        reach = jnp.minimum(
            jnp.einsum("gij,gjk->gik", reach, reach, precision=lax.Precision.HIGHEST), 1.0
        )
    return reach


def attend(queries, keys, values, mask):
    rows = queries.shape[0]
    length = keys.shape[0]
    kv_heads = keys.shape[1] // HEAD_SIZE
    repeats = queries.shape[1] // keys.shape[1]
    query_view = queries.reshape(rows, kv_heads, repeats, HEAD_SIZE)
    key_view = keys.reshape(length, kv_heads, HEAD_SIZE)
    value_view = values.reshape(length, kv_heads, HEAD_SIZE)
    scores = jnp.einsum(
        "qhrd,khd->hrqk", query_view, key_view, preferred_element_type=jnp.float32
    ) * HEAD_SIZE ** (-0.5)
    weights = jnp.exp(capped(scores, 50.0)) * mask[None, None]
    denominator = jnp.sum(weights, -1).transpose(2, 0, 1).reshape(rows, kv_heads * repeats)
    numerator = jnp.einsum(
        "hrqk,khd->qhrd",
        weights.astype(jnp.bfloat16),
        value_view,
        preferred_element_type=jnp.float32,
    )
    return (numerator.reshape(rows, kv_heads * repeats * HEAD_SIZE), denominator)


def per_device(
    hidden,
    medusa_w,
    embedding,
    cand_ids,
    tree_q,
    tree_key_value,
    prompt_key_value,
    block_group,
    block_len,
    block_empty,
    parents,
    out_weight,
    post_gain,
    resid,
):
    units = medusa_w.shape[2]
    inner = jnp.einsum(
        "rd,mdu->mru",
        hidden,
        lax.all_gather(medusa_w, "blk", axis=1, tiled=True),
        preferred_element_type=jnp.float32,
    )
    own_cols = lax.dynamic_slice_in_dim(hidden, lax.axis_index("mp") * units, units, 1).astype(
        jnp.float32
    )
    fresh = (own_cols[None] + jax.nn.silu(inner)).astype(jnp.bfloat16)
    full_fresh = lax.all_gather(fresh, "mp", axis=2, tiled=True)
    logits = capped(
        jnp.einsum("mrd,vd->mrv", full_fresh, embedding, preferred_element_type=jnp.float32), 30.0
    )
    totals = jnp.sum(jnp.exp(logits), -1)
    vocab_dev = embedding.shape[0]
    first_id = lax.axis_index(("blk", "mp")) * vocab_dev
    local_ids = cand_ids - first_id
    match = local_ids[..., None] == jnp.arange(vocab_dev, dtype=jnp.int32)
    picked = jnp.sum(jnp.where(match, logits[:, :, None, :], 0.0), -1)
    totals, picked = lax.psum((totals, picked), ("blk", "mp"))
    draft_logprob = picked - jnp.log(totals)[..., None]
    groups, tree_size, features = tree_q.shape
    keys = prompt_key_value[0, 0]
    values = prompt_key_value[1, 0]
    length = keys.shape[0]
    group = block_group[0]
    key_ok = ((jnp.arange(length, dtype=jnp.int32) < block_len[0]) & (block_empty[0] == 0)).astype(
        jnp.float32
    )
    row_group = jnp.arange(groups * tree_size, dtype=jnp.int32) // tree_size
    mask = (row_group == group).astype(jnp.float32)[:, None] * key_ok[None, :]
    numer, denom = attend(tree_q.reshape(groups * tree_size, features), keys, values, mask)
    rows_dev = groups * tree_size // lax.axis_size("blk")
    first_row = lax.axis_index("blk") * rows_dev
    summed = lax.psum((numer, denom), "blk")
    numer = lax.dynamic_slice_in_dim(summed[0], first_row, rows_dev, 0)
    denom = lax.dynamic_slice_in_dim(summed[1], first_row, rows_dev, 0)
    reach = ancestry(parents)
    tree_numer, tree_denom = jax.vmap(attend)(tree_q, tree_key_value[0], tree_key_value[1], reach)
    heads_dev = tree_denom.shape[2]
    tree_numer = lax.dynamic_slice_in_dim(
        tree_numer.reshape(groups * tree_size, features), first_row, rows_dev, 0
    )
    tree_denom = lax.dynamic_slice_in_dim(
        tree_denom.reshape(groups * tree_size, heads_dev), first_row, rows_dev, 0
    )
    numer = numer + tree_numer
    denom = denom + tree_denom
    heads_out = (
        (numer.reshape(rows_dev, heads_dev, HEAD_SIZE) / denom[..., None])
        .reshape(rows_dev, features)
        .astype(jnp.bfloat16)
    )
    attn = lax.psum(jnp.dot(heads_out, out_weight, preferred_element_type=jnp.float32), "mp")
    normed = attn * lax.rsqrt(jnp.mean(attn * attn, -1, keepdims=True) + 1e-06) * post_gain
    layer_out = (normed + resid.astype(jnp.float32)).astype(jnp.bfloat16)
    return (draft_logprob, layer_out)


def solution(mesh):
    placed = (
        P(),
        P(None, "blk", "mp"),
        P(("blk", "mp"), None),
        P(),
        P(None, None, "mp"),
        P(None, None, None, "mp"),
        P(None, "blk", None, "mp"),
        P("blk"),
        P("blk"),
        P("blk"),
        P(),
        P("mp", None),
        P(),
        P("blk", None),
    )
    return jax.shard_map(
        per_device, mesh=mesh, in_specs=placed, out_specs=(P(), P("blk", None)), check_vma=False
    )
```

profile of v0, /device:TPU:1, one launch (start us, length us, event | category | flops | bytes accessed | tf_op | source)
XLA Modules:
  0.0 381.7 jit_solution(4261685247920140671)
XLA Ops:
  7.2 0.0 all-reduce.4.cloned.1.call-start
  7.2 4.4 %fusion.51 = (bf16[1,1,2048,512]{3,2,1,0:T(8,128)(2,1)}, bf16[1,1,2048,512]{3,2,1,0:T(8,128)(2,1)}) fusion(bf16[2,1,2048,512]{3,2,1,0:T(8,128)(2,1)} %param.20), kind=kLoop, calls=%fused_computation.70 | loop fusion | bytes 8388608 | tf_op jit(solution)/shard_map/slice | solution.py:88
  11.6 2.9 copy.79
  16.5 3.3 reshape_reshape.3
  19.8 4.0 %copy.80 = bf16[1,1,2048,512]{2,3,1,0:T(8,128)(2,1)} copy(bf16[1,1,2048,512]{3,2,1,0:T(8,128)(2,1)} %get-tuple-element.6) | data formatting | bytes 4194304
  23.8 0.4 broadcast_multiply_fusion
  24.2 0.0 copy-start.1
  24.2 10.5 %fusion = (f32[2,2,576]{2,1,0:T(2,128)}, f32[2,2048,576,2]{1,2,3,0:T(8,128)}) fusion(f32[576,2048]{1,0:T(8,128)S(1)} %broadcast_multiply_fusion, bf16[2048,2,256,1]{0,2,3,1:T(8,128)(2,1)S(1)} %bitcast.83, bf16[576,2,2,256]{3,2,1,0:T(2,128)(2,1)S(1)} %reshape_reshape.3), kind=kOutput, calls=%fused_computation.1 | convolution fusion | flops 2434791168 | bytes 26878976 | tf_op jit(solution)/shard_map/qhrd,khd->hrqk/dot_general | solution.py:33
  34.7 0.0 copy-done.1
  34.7 9.1 %fusion.6 = f32[576,2,2,256]{3,0,2,1:T(8,128)S(1)} fusion(bf16[2048,2,256,1]{0,2,3,1:T(8,128)(2,1)S(1)} %bitcast.85, f32[2,2048,576,2]{1,2,3,0:T(8,128)} %get-tuple-element.15, f32[576,2048]{1,0:T(8,128)S(1)} %broadcast_multiply_fusion), kind=kOutput, calls=%fused_computation.10 | convolution fusion | flops 2434793472 | bytes 28049408 | tf_op jit(solution)/shard_map/hrqk,khd->qhrd/dot_general | solution.py:38
  43.8 1.8 copy.56
  45.6 2.9 reshape.101
  48.6 0.0 copy-start
  48.6 0.0 copy-start.2
  48.6 0.0 all-reduce.4.cloned.1.call-update
  48.6 0.0 all-gather.3.cloned.1.call-start
  48.6 0.7 all-gather.3.cloned.1.call-update
  49.3 0.2 all-reduce.6.cloned.1.call-start
  49.6 0.3 copy-done
  49.8 0.9 reshape.102
  50.7 0.7 reshape.104
  51.4 0.0 copy-done.2
  51.4 0.1 fusion.52
  51.5 0.1 reshape_squeeze.14
  51.7 1.4 convolution_minimum_fusion.5
  53.1 0.4 convolution_minimum_fusion.4
  53.5 0.4 convolution_minimum_fusion.3
  53.9 0.4 convolution_minimum_fusion.2
  54.4 0.4 convolution_minimum_fusion.1
  54.8 0.4 convolution_minimum_fusion
  55.2 0.1 copy.59
  55.3 0.9 fusion.53
  56.2 0.1 reshape.105
  56.3 124.9 %psum.38 = f32[576,4]{0,1:T(4,128)S(1)} all-reduce(f32[576,4]{0,1:T(4,128)S(1)} %reshape.104), channel_id=1, replica_groups=mesh['blk'=32,'mp'=4] {'blk'}, use_global_device_ids=true, to_apply=%region_6.7 | all-reduce | flops 2304 | bytes 18432 | tf_op jit(solution)/shard_map/psum | solution.py:99
  181.2 0.1 dynamic-slice_add_fusion
  181.3 0.1 copy.64
  181.4 0.1 div.48
  181.5 0.1 reshape_squeeze.15
  181.7 0.5 convolution_bitcast_fusion
  182.2 1.8 copy.62
  184.0 0.0 copy-start.4
  184.1 2.9 reshape.103
  187.0 0.0 copy-done.4
  187.0 0.0 all-reduce.4.cloned.1.call-done
  187.1 5.1 %fusion.39 = f32[18,3584]{1,0:T(8,128)} fusion(bf16[1024,3584]{1,0:T(8,128)(2,1)} %param.25, f32[18,1024]{1,0:T(8,128)S(1)} %bitcast.87, f32[576,1024]{1,0:T(8,128)} %reshape.103, s32[]{:T(128)S(6)} %select_n.25, f32[576,1024]{1,0:T(8,128)} %all-reduce.4.cloned.1.call-done), kind=kOutput, calls=%fused_computation.47 | convolution fusion | flops 132175872 | bytes 7868420 | tf_op jit(solution)/shard_map/dot_general | solution.py:118
  192.1 0.0 all-reduce.6.cloned.1.call-update
  192.1 0.0 copy-start.5
  192.2 0.0 copy-start.3
  192.2 0.0 copy-start.6
  192.2 0.3 all-gather.5.cloned.1.call-start
  192.4 32.7 %all-gather.3.cloned.1.call-done = bf16[2,3584,896]{2,1,0:T(8,128)(2,1)} async-done(((bf16[2,112,896]{2,1,0:T(8,128)(2,1)}), bf16[2,3584,896]{2,1,0:T(8,128)(2,1)}) %all-gather.3.cloned.1.call-update) | async-done | bytes 12845072 | tf_op jit(solution)/shard_map/all_gather | solution.py:67
  225.2 7.6 %add_convert_fusion = bf16[2,144,896]{2,1,0:T(8,128)(2,1)} fusion(bf16[2,3584,896]{2,1,0:T(8,128)(2,1)} %all-gather.3.cloned.1.call-done, bf16[144,3584]{1,0:T(8,128)(2,1)S(1)} %copy-done.4, f32[144,896]{1,0:T(8,128)S(1)} %dynamic-slice_convert_fusion), kind=kOutput, calls=%fused_computation.32 | convolution fusion | flops 1851236352 | bytes 14909440 | tf_op jit(solution)/shard_map/rd,mdu->mru/dot_general | solution.py:64
  232.8 0.0 all-gather.5.cloned.1.call-update
  232.8 0.0 copy-done.5
  232.8 34.1 %all-reduce.6.cloned.1.call-done = f32[18,3584]{1,0:T(8,128)} async-done(((f32[18,3584]{1,0:T(8,128)}), f32[18,3584]{1,0:T(8,128)}) %all-reduce.6.cloned.1.call-update) | async-done | bytes 258064 | tf_op jit(solution)/shard_map/psum | solution.py:118
  266.9 1.1 multiply_reduce_fusion
  268.0 0.0 copy-done.3
  268.0 0.0 copy-done.6
  268.0 1.8 add_convert_fusion.1
  269.8 31.7 %all-gather.5.cloned.1.call-done = bf16[2,144,3584]{2,1,0:T(8,128)(2,1)} async-done(((bf16[2,144,896]{2,1,0:T(8,128)(2,1)}), bf16[2,144,3584]{2,1,0:T(8,128)(2,1)}) %all-gather.5.cloned.1.call-update) | async-done | bytes 2064400 | tf_op jit(solution)/shard_map/all_gather | solution.py:74
  301.5 6.2 %exponential_reduce_fusion = (f32[2,144]{1,0:T(2,128)S(1)}, f32[2,144,1024]{2,1,0:T(8,128)S(1)}) fusion(bf16[2,144,3584]{2,1,0:T(8,128)(2,1)} %all-gather.5.cloned.1.call-done, bf16[1024,3584]{1,0:T(8,128)(2,1)} %param.16), kind=kOutput, calls=%fused_computation.24 | convolution fusion | flops 2114813696 | bytes 10585216 | tf_op jit(solution)/shard_map/mrd,vd->mrv/dot_general | solution.py:76
  307.8 1.8 select_reduce_fusion
  309.6 64.9 %all-reduce = (f32[2,144,10]{1,2,0:T(8,128)S(1)}, f32[2,144]{1,0:T(2,128)S(1)}) all-reduce(f32[2,144,10]{1,2,0:T(8,128)S(1)} %select_reduce_fusion, f32[2,144]{1,0:T(2,128)S(1)} %get-tuple-element.10), channel_id=1, replica_groups=mesh['blk'=32,'mp'=4] {'blk','mp'}, use_global_device_ids=true, to_apply=%region_1.2 | all-reduce | flops 3168 | bytes 25344 | tf_op jit(solution)/shard_map/psum | solution.py:84
  374.5 0.6 copy.65
  (13 shorter events, 0.1 us)
Async XLA Ops:
  7.2 179.9 %all-reduce.4.cloned.1.call-start = ((), (), s32[]{:S(2)}) async-start(), calls=%async_computation.2 | async-start | bytes 4718592 | tf_op jit(solution)/shard_map/psum | solution.py:99
  24.2 10.5 %copy-start.1 = (bf16[1,1,2048,512]{2,3,1,0:T(8,128)(2,1)S(1)}, bf16[1,1,2048,512]{2,3,1,0:T(8,128)(2,1)}, u32[]{:S(2)}) copy-start(bf16[1,1,2048,512]{2,3,1,0:T(8,128)(2,1)} %copy.80) | copy-start | bytes 6291460
  48.6 1.3 copy-start
  48.6 2.9 copy-start.2
  48.6 176.6 %all-gather.3.cloned.1.call-start = ((), (), s32[]{:S(2)}) async-start(), calls=%async_computation | async-start | bytes 13246464 | tf_op jit(solution)/shard_map/all_gather | solution.py:67
  49.3 217.6 %all-reduce.6.cloned.1.call-start = ((), (), s32[]{:S(2)}) async-start(), calls=%async_computation.3 | async-start | bytes 688128 | tf_op jit(solution)/shard_map/psum | solution.py:118
  184.0 3.0 copy-start.4
  192.1 40.7 %copy-start.5 = (s32[2,144,10]{1,0,2:T(2,128)S(1)}, s32[2,144,10]{1,0,2:T(2,128)}, u32[]{:S(2)}) copy-start(s32[2,144,10]{1,0,2:T(2,128)} %param.17) | copy-start | bytes 34564
  192.2 75.9 %copy-start.3 = (bf16[18,3584]{1,0:T(8,128)(2,1)S(1)}, bf16[18,3584]{1,0:T(8,128)(2,1)}, u32[]{:S(2)}) copy-start(bf16[18,3584]{1,0:T(8,128)(2,1)} %param.27) | copy-start | bytes 387076
  192.2 75.9 %copy-start.6 = (f32[3584]{0:T(1024)S(1)}, f32[3584]{0:T(1024)}, u32[]{:S(2)}) copy-start(f32[3584]{0:T(1024)} %param.26) | copy-start | bytes 43012
  192.2 109.4 %all-gather.5.cloned.1.call-start = ((), (), s32[]{:S(2)}) async-start(), calls=%async_computation.1 | async-start | bytes 2580480 | tf_op jit(solution)/shard_map/all_gather | solution.py:74
Sparse Core Ops, SparseCore 0:
  48.7 110.4 all-reduce.3
  161.6 63.5 all-gather.2
  227.5 39.3 all-reduce.5
  268.4 33.0 all-gather.4
where the time goes:
time: 382 us
  blocking collectives  190 us (50%)
  waiting for transfers between devices  99.3 us (26%)
  matrix products  43.3 us (11%)
  local copies, waits for them, and re-layouts  27.5 us (7%)
  between operations  16 us (4%)
  other arithmetic  5.25 us (1%)
    psum x1, blocking collectives, per_device(): summed = lax.psum((numer, denom), 'blk')  125 us
    psum x1, blocking collectives, per_device(): totals, picked = lax.psum((totals, picked), ('blk', 'mp'))  64.9 us
    psum x1, waiting for transfers between devices, per_device(): lax.psum(jnp.dot(heads_out, out_weight, preferred_element_type=jnp.float3...  34.1 us
    all_gather x1, waiting for transfers between devices, per_device(): lax.all_gather(medusa_w, 'blk', axis=1, tiled=True)  32.7 us
    all_gather x1, waiting for transfers between devices, per_device(): full_fresh = lax.all_gather(fresh, 'mp', axis=2, tiled=True)  31.7 us
    dot_general x2, matrix products, attend(): jnp.einsum('qhrd,khd->hrqk', query_view, key_view, preferred_element_type...  11.3 us
    dot_general x2, matrix products, attend(): jnp.einsum('hrqk,khd->qhrd', weights.astype(jnp.bfloat16), value_view, pr...  9.63 us
    unnamed x19, local copies, waits for them, and re-layouts  7.84 us
  transfers between devices with their start and end apart: 4, of which 3 were waited for; matrix products, arithmetic and copies ran while one was open for 7% of the time, Pallas kernels for 0%

commit v1 on v0

--- a/solution.py
+++ b/solution.py
@@ -81,7 +81,7 @@
     local_ids = cand_ids - first_id
     match = local_ids[..., None] == jnp.arange(vocab_dev, dtype=jnp.int32)
     picked = jnp.sum(jnp.where(match, logits[:, :, None, :], 0.0), -1)
-    totals, picked = lax.psum((totals, picked), ("blk", "mp"))
+    totals, picked = lax.psum(lax.psum((totals, picked), "mp"), "blk")
     draft_logprob = picked - jnp.log(totals)[..., None]
     groups, tree_size, features = tree_q.shape
     keys = prompt_key_value[0, 0]

time: 382 us -> 341 us (0.89)
  blocking collectives: 190 us -> 136 us
  other arithmetic: 5.25 us -> 9.69 us
    psum x2, blocking collectives: 190 us -> 136 us  [per_device(): totals, picked = lax.psum(lax.psum((totals, picked), 'mp'), 'blk')]
    all_gather x1, waiting for transfers between devices: 31.7 us -> 0.01 us  [per_device(): full_fresh = lax.all_gather(fresh, 'mp', axis=2, tiled=True)]
    all_gather x1, waiting for transfers between devices: 32.7 us -> 61.9 us  [per_device(): lax.all_gather(medusa_w, 'blk', axis=1, tiled=True)]
    psum x1, waiting for transfers between devices: 34.1 us -> 39 us  [per_device(): lax.psum(jnp.dot(heads_out, out_weight, preferred_element_type=jnp.float3...]
    unnamed x19 -> x23, local copies, waits for them, and re-layouts: 7.84 us -> 8.09 us
  transfers between devices with their start and end apart: 4 -> 4, of which waited for: 3 -> 2; matrix products, arithmetic and copies ran while one was open for 7% -> 20% of each run, Pallas kernels for 0% -> 0%
where the time goes in v1:
time: 341 us; the launch traced here: 339 us
  blocking collectives  136 us (40%)
  waiting for transfers between devices  102 us (30%)
  matrix products  45.2 us (13%)
  local copies, waits for them, and re-layouts  29.1 us (9%)
  between operations  16 us (5%)
  other arithmetic  9.69 us (3%)
    psum x2, blocking collectives, per_device(): totals, picked = lax.psum(lax.psum((totals, picked), 'mp'), 'blk')  136 us
    all_gather x1, waiting for transfers between devices, per_device(): lax.all_gather(medusa_w, 'blk', axis=1, tiled=True)  61.9 us
    psum x1, waiting for transfers between devices, per_device(): lax.psum(jnp.dot(heads_out, out_weight, preferred_element_type=jnp.float3...  39 us
    dot_general x2, matrix products, attend(): jnp.einsum('qhrd,khd->hrqk', query_view, key_view, preferred_element_type...  13.1 us
    dot_general x2, matrix products, attend(): jnp.einsum('hrqk,khd->qhrd', weights.astype(jnp.bfloat16), value_view, pr...  9.6 us
    unnamed x23, local copies, waits for them, and re-layouts  8.09 us
    dot_general x1, matrix products, per_device(): jnp.einsum('rd,mdu->mru', hidden, lax.all_gather(medusa_w, 'blk', axis=1,...  7.56 us
  transfers between devices with their start and end apart: 4, of which 2 were waited for; matrix products, arithmetic and copies ran while one was open for 20% of the time, Pallas kernels for 0%

profile of v1, /device:TPU:1, one launch (start us, length us, event | category | flops | bytes accessed | tf_op | source)
XLA Modules:
  0.0 338.5 jit_solution(17115979084939883729)
XLA Ops:
  7.2 0.0 all-gather.3.cloned.1.call-start
  7.2 0.7 all-gather.3.cloned.1.call-update
  7.9 0.0 all-gather.5.cloned.1.call-start
  9.9 1.0 dynamic-slice_convert_fusion
  10.9 0.0 copy-start.5
  10.9 4.5 %fusion.51 = (bf16[1,1,2048,512]{3,2,1,0:T(8,128)(2,1)}, bf16[1,1,2048,512]{3,2,1,0:T(8,128)(2,1)}) fusion(bf16[2,1,2048,512]{3,2,1,0:T(8,128)(2,1)} %param.20), kind=kLoop, calls=%fused_computation.70 | loop fusion | bytes 8388608 | tf_op jit(solution)/shard_map/slice | solution.py:88
  15.4 61.9 %all-gather.3.cloned.1.call-done = bf16[2,3584,896]{2,1,0:T(8,128)(2,1)} async-done(((bf16[2,112,896]{2,1,0:T(8,128)(2,1)}), bf16[2,3584,896]{2,1,0:T(8,128)(2,1)}) %all-gather.3.cloned.1.call-update) | async-done | bytes 12845072 | tf_op jit(solution)/shard_map/all_gather | solution.py:67
  77.3 0.0 copy-done.5
  77.3 7.6 %add_convert_fusion = bf16[2,144,896]{2,1,0:T(8,128)(2,1)} fusion(bf16[2,3584,896]{2,1,0:T(8,128)(2,1)} %all-gather.3.cloned.1.call-done, bf16[144,3584]{1,0:T(8,128)(2,1)S(1)} %copy-done.5, f32[144,896]{1,0:T(8,128)S(1)} %dynamic-slice_convert_fusion), kind=kOutput, calls=%fused_computation.32 | convolution fusion | flops 1851236352 | bytes 14909440 | tf_op jit(solution)/shard_map/rd,mdu->mru/dot_general | solution.py:64
  84.8 0.0 all-gather.5.cloned.1.call-update
  84.9 0.2 all-reduce.5.cloned.1.call-start
  85.1 2.5 broadcast_multiply_fusion
  87.6 2.9 copy.79
  90.6 4.0 %reshape_reshape.3 = bf16[576,2,2,256]{3,2,1,0:T(2,128)(2,1)} reshape(bf16[12,48,1024]{2,1,0:T(8,128)(2,1)} %param.18) | data formatting | bytes 2359296 | tf_op jit(solution)/shard_map/reshape;reshape | solution.py:30
  94.6 4.1 %copy.80 = bf16[1,1,2048,512]{2,3,1,0:T(8,128)(2,1)} copy(bf16[1,1,2048,512]{3,2,1,0:T(8,128)(2,1)} %get-tuple-element.9) | data formatting | bytes 4194304
  98.7 12.2 %fusion = (f32[2,2,576]{2,1,0:T(2,128)}, f32[2,2048,576,2]{1,2,3,0:T(8,128)}) fusion(f32[576,2048]{1,0:T(8,128)} %broadcast_multiply_fusion, bf16[2048,2,256,1]{0,2,3,1:T(8,128)(2,1)S(1)} %bitcast.85, bf16[576,2,2,256]{3,2,1,0:T(2,128)(2,1)} %reshape_reshape.3), kind=kOutput, calls=%fused_computation.1 | convolution fusion | flops 2434791168 | bytes 26878976 | tf_op jit(solution)/shard_map/qhrd,khd->hrqk/dot_general | solution.py:33
  110.9 0.0 slice-done
  110.9 0.0 slice-done.1
  110.9 0.0 copy-done.1
  110.9 9.1 %fusion.6 = f32[576,2,2,256]{3,0,2,1:T(8,128)S(1)} fusion(bf16[2048,2,256,1]{0,2,3,1:T(8,128)(2,1)S(1)} %bitcast.87, f32[2,2048,576,2]{1,2,3,0:T(8,128)} %get-tuple-element.16, f32[576,2048]{1,0:T(8,128)S(1)} %bitcast.84), kind=kOutput, calls=%fused_computation.10 | convolution fusion | flops 2434793472 | bytes 28049408 | tf_op jit(solution)/shard_map/hrqk,khd->qhrd/dot_general | solution.py:38
  120.0 1.8 copy.56
  121.8 2.9 reshape.101
  124.7 0.0 all-reduce.5.cloned.1.call-update
  124.8 0.3 all-reduce.7.cloned.1.call-start
  125.0 0.6 fusion.40
  125.6 0.4 copy-done
  126.0 0.9 reshape.102
  126.9 0.7 broadcast_subtract_fusion.1
  127.7 0.6 copy.50
  128.3 0.7 reshape.104
  129.0 0.0 copy-done.2
  129.0 0.1 fusion.52
  129.1 0.1 reshape_squeeze.14
  129.2 1.4 convolution_minimum_fusion.5
  130.6 0.4 convolution_minimum_fusion.4
  131.1 0.4 convolution_minimum_fusion.3
  131.5 0.4 convolution_minimum_fusion.2
  131.9 0.4 convolution_minimum_fusion.1
  132.3 0.4 convolution_minimum_fusion
  132.8 0.1 copy.59
  132.9 0.9 fusion.53
  133.8 0.1 reshape.105
  133.9 0.1 reshape_squeeze.15
  134.0 0.5 convolution_bitcast_fusion
  134.6 1.8 copy.62
  136.4 2.9 reshape.103
  139.4 6.4 %exponential_reduce_fusion = (f32[2,144]{1,0:T(2,128)S(1)}, f32[2,144,1024]{2,1,0:T(8,128)S(1)}) fusion(bf16[2,144,3584]{2,1,0:T(8,128)(2,1)} %all-gather.5.cloned.1.call-done, bf16[1024,3584]{1,0:T(8,128)(2,1)} %param.16), kind=kOutput, calls=%fused_computation.24 | convolution fusion | flops 2114813696 | bytes 10585216 | tf_op jit(solution)/shard_map/mrd,vd->mrv/dot_general | solution.py:76
  145.7 0.0 copy-done.4
  145.7 1.8 select_reduce_fusion
  147.6 14.1 %all-reduce.1 = (f32[2,144,10]{1,2,0:T(8,128)S(1)}, f32[2,144]{1,0:T(2,128)S(1)}) all-reduce(f32[2,144,10]{1,2,0:T(8,128)S(1)} %select_reduce_fusion, f32[2,144]{1,0:T(2,128)S(1)} %get-tuple-element.13), channel_id=1, replica_groups=mesh['blk'=32,'mp'=4] {'mp'}, use_global_device_ids=true, to_apply=%region_1.2 | all-reduce | flops 3168 | bytes 25344 | tf_op jit(solution)/shard_map/psum | solution.py:84
  161.7 122.2 %all-reduce = (f32[2,144,10]{1,2,0:T(8,128)S(1)}, f32[2,144]{1,0:T(2,128)S(1)}, f32[576,4]{0,1:T(4,128)S(1)}) all-reduce(f32[2,144,10]{1,2,0:T(8,128)S(1)} %get-tuple-element.7, f32[2,144]{1,0:T(2,128)S(1)} %get-tuple-element.8, f32[576,4]{0,1:T(4,128)S(1)} %reshape.104), channel_id=1, replica_groups=mesh['blk'=32,'mp'=4] {'blk'}, use_global_device_ids=true, to_apply=%region_2.3 | all-reduce | flops 5472 | bytes 43776 | tf_op jit(solution)/shard_map/psum | solution.py:84
  283.9 0.1 dynamic-slice_add_fusion
  284.0 0.1 copy.64
  284.1 0.1 div.48
  284.2 0.0 all-reduce.5.cloned.1.call-done
  284.3 0.0 copy-start.3
  284.3 0.0 copy-start.6
  284.3 5.1 %fusion.39 = f32[18,3584]{1,0:T(8,128)} fusion(bf16[1024,3584]{1,0:T(8,128)(2,1)} %param.25, f32[18,1024]{1,0:T(8,128)S(1)} %bitcast.89, f32[576,1024]{1,0:T(8,128)} %reshape.103, s32[]{:T(128)S(6)} %select_n.25, f32[576,1024]{1,0:T(8,128)} %all-reduce.5.cloned.1.call-done), kind=kOutput, calls=%fused_computation.47 | convolution fusion | flops 132175872 | bytes 7868420 | tf_op jit(solution)/shard_map/dot_general | solution.py:118
  289.4 0.0 all-reduce.7.cloned.1.call-update
  289.5 0.6 copy.65
  290.1 39.0 %all-reduce.7.cloned.1.call-done = f32[18,3584]{1,0:T(8,128)} async-done(((f32[18,3584]{1,0:T(8,128)}), f32[18,3584]{1,0:T(8,128)}) %all-reduce.7.cloned.1.call-update) | async-done | bytes 258064 | tf_op jit(solution)/shard_map/psum | solution.py:118
  329.1 1.1 multiply_reduce_fusion
  330.2 0.0 copy-done.3
  330.2 1.8 add_convert_fusion.1
  (18 shorter events, 0.1 us)
Async XLA Ops:
  7.2 70.1 %all-gather.3.cloned.1.call-start = ((), (), s32[]{:S(2)}) async-start(), calls=%async_computation | async-start | bytes 13246464 | tf_op jit(solution)/shard_map/all_gather | solution.py:67
  7.9 131.5 %all-gather.5.cloned.1.call-start = ((), (), s32[]{:S(2)}) async-start(), calls=%async_computation.1 | async-start | bytes 2580480 | tf_op jit(solution)/shard_map/all_gather | solution.py:74
  10.9 66.4 %copy-start.5 = (bf16[144,3584]{1,0:T(8,128)(2,1)S(1)}, bf16[144,3584]{1,0:T(8,128)(2,1)}, u32[]{:S(2)}) copy-start(bf16[144,3584]{1,0:T(8,128)(2,1)} %param.14) | copy-start | bytes 3096580
  84.9 199.4 %all-reduce.5.cloned.1.call-start = ((), (), s32[]{:S(2)}) async-start(), calls=%async_computation.2 | async-start | bytes 4718592 | tf_op jit(solution)/shard_map/psum | solution.py:99
  94.6 16.3 %slice-start = ((s8[4718592]{0:T(1024)(128)(4,1)}), s8[524288]{0:T(1024)(128)(4,1)S(1)}, s32[]{:S(2)}) async-start(s8[4718592]{0:T(1024)(128)(4,1)} %bitcast.83), calls=%async_computation.4 | async-start | bytes 1048576
  98.7 12.2 %slice-start.1 = ((s8[4718592]{0:T(1024)(128)(4,1)}), s8[4194304]{0:T(1024)(128)(4,1)S(1)}, s32[]{:S(2)}) async-start(s8[4718592]{0:T(1024)(128)(4,1)} %bitcast.83), calls=%async_computation.5 | async-start | bytes 8388608
  98.7 12.2 %copy-start.1 = (bf16[1,1,2048,512]{2,3,1,0:T(8,128)(2,1)S(1)}, bf16[1,1,2048,512]{2,3,1,0:T(8,128)(2,1)}, u32[]{:S(2)}) copy-start(bf16[1,1,2048,512]{2,3,1,0:T(8,128)(2,1)} %copy.80) | copy-start | bytes 6291460
  124.7 1.3 copy-start
  124.7 4.3 %copy-start.2 = (bf16[2,12,48,512]{3,2,1,0:T(8,128)(2,1)S(1)}, bf16[2,12,48,512]{3,2,1,0:T(8,128)(2,1)}, u32[]{:S(2)}) copy-start(bf16[2,12,48,512]{3,2,1,0:T(8,128)(2,1)} %param.19) | copy-start | bytes 3538948
  124.8 204.3 %all-reduce.7.cloned.1.call-start = ((), (), s32[]{:S(2)}) async-start(), calls=%async_computation.3 | async-start | bytes 688128 | tf_op jit(solution)/shard_map/psum | solution.py:118
  139.3 6.4 %copy-start.4 = (s32[2,144,10]{1,2,0:T(8,128)S(1)}, s32[2,144,10]{1,2,0:T(8,128)}, u32[]{:S(2)}) copy-start(s32[2,144,10]{1,2,0:T(8,128)} %copy.50) | copy-start | bytes 34564
  284.3 45.9 %copy-start.3 = (bf16[18,3584]{1,0:T(8,128)(2,1)S(1)}, bf16[18,3584]{1,0:T(8,128)(2,1)}, u32[]{:S(2)}) copy-start(bf16[18,3584]{1,0:T(8,128)(2,1)} %param.27) | copy-start | bytes 387076
  284.3 45.9 %copy-start.6 = (f32[3584]{0:T(1024)S(1)}, f32[3584]{0:T(1024)}, u32[]{:S(2)}) copy-start(f32[3584]{0:T(1024)} %param.26) | copy-start | bytes 43012
Sparse Core Ops, SparseCore 0:
  10.4 66.8 all-gather.2
  85.0 29.9 all-gather.4
  124.9 106.3 all-reduce.4
  289.5 39.4 all-reduce.6
